TPU v7x, 32 devices: a whole 2x2x4 slice. The times are simulated.
32 devices in a mesh: fsdp: 8 (over y, x, core), sp: 4 (over z).
Axes of the slice: x: 2, y: 2, z: 4, core: 2. Of those that a mesh axis runs over, the one named last changes fastest.
Arguments:
- inputs: bfloat16 [16, 1024, 768], P('fsdp', 'sp'), may hold values from -6 to 6
- block_ids: int32 [16, 1024], P('fsdp', 'sp'), may hold values from 0 to 3, never falling along the last dimension, each value on 1 to 512 neighbouring positions
- first_gain: bfloat16 [768], P('fsdp'), may hold values from 0.5 to 1.5
- first_shift: bfloat16 [768], P('fsdp'), may hold values from -3 to 3
- w_project: bfloat16 [768, 2304], P('fsdp'), may hold values from -0.21875 to 0.21875
- query_bias: bfloat16 [768], P('fsdp'), may hold values from -3 to 3
- value_bias: bfloat16 [768], P('fsdp'), may hold values from -3 to 3
- w_output: bfloat16 [768, 768], P('fsdp'), may hold values from -4 to 4
- output_bias: bfloat16 [768], P('fsdp'), may hold values from -3 to 3
- second_gain: bfloat16 [768], P('fsdp'), may hold values from 0.5 to 1.5
- second_shift: bfloat16 [768], P('fsdp'), may hold values from -3 to 3
- w_expand: bfloat16 [768, 3072], P('fsdp'), may hold values from -0.21875 to 0.21875
- expand_bias: bfloat16 [3072], P('fsdp'), may hold values from -3 to 3
- w_reduce: bfloat16 [3072, 768], P('fsdp'), may hold values from -0.109375 to 0.109375
- reduce_bias: bfloat16 [768], P('fsdp'), may hold values from -3 to 3
- out_grad: bfloat16 [16, 1024, 768], P('fsdp', 'sp'), may hold values from -6 to 6
Outputs:
- layer_output: bfloat16 [16, 1024, 768], P('fsdp', 'sp')
- input_grad: float32 [16, 1024, 768], P('fsdp', 'sp')
- grad_first_gain: float32 [768], P('fsdp')
- grad_first_shift: float32 [768], P('fsdp')
- grad_project: float32 [768, 2304], P('fsdp')
- grad_query_bias: float32 [768], P('fsdp')
- grad_value_bias: float32 [768], P('fsdp')
- grad_output: float32 [768, 768], P('fsdp')
- grad_output_bias: float32 [768], P('fsdp')
- grad_second_gain: float32 [768], P('fsdp')
- grad_second_shift: float32 [768], P('fsdp')
- grad_expand: float32 [768, 3072], P('fsdp')
- grad_expand_bias: float32 [3072], P('fsdp')
- grad_reduce: float32 [3072, 768], P('fsdp')
- grad_reduce_bias: float32 [768], P('fsdp')
Inputs may be any that keep to these rules, and one draw needn't show every extreme that they name: `block_ids`: block numbers never fall along a sequence, and every number from 0 to 3 occurs in each sequence.
All inputs are finite; a program needn't handle non-finite values.
Results may differ from a plain program's by a relative error of at most 0.011.
Values may be sent and summed in bfloat16 or wider, within the bound.
No kernel may reach another device: no remote copies, remote signals or barrier semaphores. Data moves between devices by JAX's collectives and lax.ppermute only.
A program may use at most 192 MiB of HBM per device.

v0:
```python
import math
import jax
import jax.numpy as jnp
from jax import lax
from jax.sharding import PartitionSpec as P

H = 12
HD = 64
EPSILON = 1e-05
GELU_C = 0.7978845608028654
GELU_A = 0.044715
MASKED = -1e30


def norm_forward(rows, gain, shift):
    average = jnp.mean(rows, axis=-1, keepdims=True)
    centered = rows - average
    variance = jnp.mean(centered * centered, axis=-1, keepdims=True)
    inv_std = lax.rsqrt(variance + EPSILON)
    normed = centered * inv_std
    return (normed, inv_std, normed * gain + shift)


def norm_backward(grad_rows, normed, inv_std, gain):
    scaled = grad_rows * gain
    first_mean = jnp.mean(scaled, axis=-1, keepdims=True)
    second_mean = jnp.mean(scaled * normed, axis=-1, keepdims=True)
    grad_in = inv_std * (scaled - first_mean - normed * second_mean)
    return (grad_in, jnp.sum(grad_rows * normed, axis=0), jnp.sum(grad_rows, axis=0))


def gelu_parts(pre):
    tangent = jnp.tanh(GELU_C * (pre + GELU_A * pre * pre * pre))
    value = 0.5 * pre * (1.0 + tangent)
    slope = 0.5 * (1.0 + tangent) + 0.5 * pre * (1.0 - tangent * tangent) * GELU_C * (
        1.0 + 3.0 * GELU_A * pre * pre
    )
    return (value, slope)


def contract(left, right, left_dim, right_dim):
    return lax.dot_general(
        left, right, (((left_dim,), (right_dim,)), ((), ())), preferred_element_type=jnp.float32
    )


def masked_scores(query, keys, blocks, scale):
    raw = jnp.einsum("hdq,hdk->hqk", query, keys, preferred_element_type=jnp.float32) * scale
    allowed = blocks[None, :] <= blocks[:, None]
    return jnp.where(allowed[None], raw, MASKED)


def per_device(
    inputs,
    block_ids,
    first_gain,
    first_shift,
    w_project,
    query_bias,
    value_bias,
    w_output,
    output_bias,
    second_gain,
    second_shift,
    w_expand,
    expand_bias,
    w_reduce,
    reduce_bias,
    out_grad,
):
    seq_dev, local, width = inputs.shape
    rows = seq_dev * local
    groups = lax.axis_size("sp")
    per_dev = H // groups
    group_width = per_dev * HD
    length = local * groups
    scale = 1.0 / math.sqrt(HD)
    f32 = jnp.float32
    bf16 = jnp.bfloat16
    (
        gain_one,
        shift_one,
        proj_full,
        qbias_full,
        vbias_full,
        out_full,
        obias_full,
        gain_two,
        shift_two,
        exp_full,
        ebias_full,
        red_full,
        rbias_full,
    ) = (
        lax.all_gather(first_gain, "fsdp", axis=0, tiled=True),
        lax.all_gather(first_shift, "fsdp", axis=0, tiled=True),
        lax.all_gather(w_project, "fsdp", axis=0, tiled=True),
        lax.all_gather(query_bias, "fsdp", axis=0, tiled=True),
        lax.all_gather(value_bias, "fsdp", axis=0, tiled=True),
        lax.all_gather(w_output, "fsdp", axis=0, tiled=True),
        lax.all_gather(output_bias, "fsdp", axis=0, tiled=True),
        lax.all_gather(second_gain, "fsdp", axis=0, tiled=True),
        lax.all_gather(second_shift, "fsdp", axis=0, tiled=True),
        lax.all_gather(w_expand, "fsdp", axis=0, tiled=True),
        lax.all_gather(expand_bias, "fsdp", axis=0, tiled=True),
        lax.all_gather(w_reduce, "fsdp", axis=0, tiled=True),
        lax.all_gather(reduce_bias, "fsdp", axis=0, tiled=True),
    )
    blocks = lax.all_gather(block_ids, "sp", axis=1, tiled=True)
    resid = inputs.astype(f32).reshape(rows, width)
    normed_one, inv_one, pre_one = norm_forward(resid, gain_one.astype(f32), shift_one.astype(f32))
    normed_in = pre_one.astype(bf16)
    bias_all = jnp.concatenate([qbias_full, jnp.zeros_like(qbias_full), vbias_full]).astype(f32)
    proj_t = contract(proj_full, normed_in, 0, 1) + bias_all[:, None]
    proj_low = proj_t.astype(bf16).reshape(3, groups, group_width, seq_dev, local)
    heads = lax.all_to_all(proj_low, "sp", split_axis=1, concat_axis=4, tiled=True)
    per_seq = jnp.transpose(heads.reshape(3, per_dev, HD, seq_dev, length), (3, 0, 1, 2, 4))

    def attend(item):
        triple, seq_blocks = item
        scores = masked_scores(triple[0], triple[1], seq_blocks, scale)
        peak = jnp.max(scores, axis=-1, keepdims=True)
        raised = jnp.exp(scores - peak)
        summed = jnp.sum(raised, axis=-1, keepdims=True)
        attn_prob = (raised / summed).astype(bf16)
        mixed = jnp.einsum("hqk,hdk->hdq", attn_prob, triple[2], preferred_element_type=f32)
        return (mixed.astype(bf16), peak + jnp.log(summed))

    mixed_all, log_norm = lax.map(attend, (per_seq, blocks))
    mixed_t = jnp.transpose(mixed_all, (1, 2, 0, 3)).reshape(group_width, seq_dev, groups, local)
    attended = lax.all_to_all(mixed_t, "sp", split_axis=2, concat_axis=0, tiled=True).reshape(
        width, rows
    )
    middle = resid + (contract(attended, out_full, 0, 0) + obias_full.astype(f32))
    normed_two, inv_two, pre_two = norm_forward(middle, gain_two.astype(f32), shift_two.astype(f32))
    normed_mid = pre_two.astype(bf16)
    hidden = jnp.dot(normed_mid, exp_full, preferred_element_type=f32) + ebias_full.astype(f32)
    active_val, slope = gelu_parts(hidden)
    active = active_val.astype(bf16)
    result = middle + (
        jnp.dot(active, red_full, preferred_element_type=f32) + rbias_full.astype(f32)
    )
    layer_output = result.astype(bf16).reshape(seq_dev, local, width)
    gain_back, proj_back, out_back, gain_mid_back, exp_back, red_back = (
        lax.all_gather(first_gain, "fsdp", axis=0, tiled=True),
        lax.all_gather(w_project, "fsdp", axis=0, tiled=True),
        lax.all_gather(w_output, "fsdp", axis=0, tiled=True),
        lax.all_gather(second_gain, "fsdp", axis=0, tiled=True),
        lax.all_gather(w_expand, "fsdp", axis=0, tiled=True),
        lax.all_gather(w_reduce, "fsdp", axis=0, tiled=True),
    )
    grad_top = out_grad.reshape(rows, width)
    grad_red = contract(active, grad_top, 0, 0)
    grad_rbias = jnp.sum(grad_top, axis=0, dtype=f32)
    grad_active = contract(grad_top, red_back, 1, 1)
    grad_hidden = (grad_active * slope).astype(bf16)
    grad_exp = contract(normed_mid, grad_hidden, 0, 0)
    grad_ebias = jnp.sum(grad_hidden, axis=0, dtype=f32)
    grad_norm_two = contract(grad_hidden, exp_back, 1, 1)
    grad_mid_norm, grad_gain_two, grad_shift_two = norm_backward(
        grad_norm_two, normed_two, inv_two, gain_mid_back.astype(f32)
    )
    grad_middle = grad_top.astype(f32) + grad_mid_norm
    grad_branch = grad_middle.astype(bf16)
    grad_out = contract(attended, grad_branch, 1, 0)
    grad_obias = jnp.sum(grad_branch, axis=0, dtype=f32)
    grad_attn_t = (
        contract(out_back, grad_branch, 1, 1).astype(bf16).reshape(width, seq_dev, 1, local)
    )
    grad_heads = lax.all_to_all(grad_attn_t, "sp", split_axis=0, concat_axis=2, tiled=True)
    grad_seq = jnp.transpose(grad_heads.reshape(per_dev, HD, seq_dev, length), (2, 0, 1, 3))

    def attend_back(item):
        triple, seq_blocks, seq_norm, grad_mix = item
        scores = masked_scores(triple[0], triple[1], seq_blocks, scale)
        attn_prob = jnp.exp(scores - seq_norm)
        prob_low = attn_prob.astype(bf16)
        grad_values = jnp.einsum("hqk,hdq->hdk", prob_low, grad_mix, preferred_element_type=f32)
        grad_prob = jnp.einsum("hdq,hdk->hqk", grad_mix, triple[2], preferred_element_type=f32)
        centre = jnp.sum(grad_prob * attn_prob, axis=-1, keepdims=True)
        grad_scores = (attn_prob * (grad_prob - centre)).astype(bf16)
        grad_query = (
            jnp.einsum("hqk,hdk->hdq", grad_scores, triple[1], preferred_element_type=f32) * scale
        )
        grad_keys = (
            jnp.einsum("hqk,hdq->hdk", grad_scores, triple[0], preferred_element_type=f32) * scale
        )
        return jnp.stack([grad_query, grad_keys, grad_values]).astype(bf16)

    grad_triple = lax.map(attend_back, (per_seq, blocks, log_norm, grad_seq))
    grad_proj_heads = jnp.transpose(grad_triple, (1, 2, 3, 0, 4)).reshape(
        3, 1, group_width, seq_dev, length
    )
    grad_proj_t = lax.all_to_all(
        grad_proj_heads, "sp", split_axis=4, concat_axis=1, tiled=True
    ).reshape(3 * width, rows)
    grad_proj = contract(normed_in, grad_proj_t, 0, 1)
    grad_qbias = jnp.sum(grad_proj_t[:width], axis=1, dtype=f32)
    grad_vbias = jnp.sum(grad_proj_t[2 * width :], axis=1, dtype=f32)
    grad_norm_one = contract(grad_proj_t, proj_back, 0, 1)
    grad_in_norm, grad_gain_one, grad_shift_one = norm_backward(
        grad_norm_one, normed_one, inv_one, gain_back.astype(f32)
    )
    input_grad = (grad_middle + grad_in_norm).reshape(seq_dev, local, width)
    owned = (
        lax.psum_scatter(grad_gain_one, "fsdp", scatter_dimension=0, tiled=True),
        lax.psum_scatter(grad_shift_one, "fsdp", scatter_dimension=0, tiled=True),
        lax.psum_scatter(grad_proj, "fsdp", scatter_dimension=0, tiled=True),
        lax.psum_scatter(grad_qbias, "fsdp", scatter_dimension=0, tiled=True),
        lax.psum_scatter(grad_vbias, "fsdp", scatter_dimension=0, tiled=True),
        lax.psum_scatter(grad_out, "fsdp", scatter_dimension=0, tiled=True),
        lax.psum_scatter(grad_obias, "fsdp", scatter_dimension=0, tiled=True),
        lax.psum_scatter(grad_gain_two, "fsdp", scatter_dimension=0, tiled=True),
        lax.psum_scatter(grad_shift_two, "fsdp", scatter_dimension=0, tiled=True),
        lax.psum_scatter(grad_exp, "fsdp", scatter_dimension=0, tiled=True),
        lax.psum_scatter(grad_ebias, "fsdp", scatter_dimension=0, tiled=True),
        lax.psum_scatter(grad_red, "fsdp", scatter_dimension=0, tiled=True),
        lax.psum_scatter(grad_rbias, "fsdp", scatter_dimension=0, tiled=True),
    )
    (
        sum_gain_one,
        sum_shift_one,
        sum_proj,
        sum_qbias,
        sum_vbias,
        sum_out,
        sum_obias,
        sum_gain_two,
        sum_shift_two,
        sum_exp,
        sum_ebias,
        sum_red,
        sum_rbias,
    ) = lax.psum(
        (
            owned[0],
            owned[1],
            owned[2],
            owned[3],
            owned[4],
            owned[5],
            owned[6],
            owned[7],
            owned[8],
            owned[9],
            owned[10],
            owned[11],
            owned[12],
        ),
        "sp",
    )
    return (
        layer_output,
        input_grad,
        sum_gain_one,
        sum_shift_one,
        sum_proj,
        sum_qbias,
        sum_vbias,
        sum_out,
        sum_obias,
        sum_gain_two,
        sum_shift_two,
        sum_exp,
        sum_ebias,
        sum_red,
        sum_rbias,
    )


def solution(mesh):
    return jax.shard_map(
        per_device,
        mesh=mesh,
        in_specs=(
            P("fsdp", "sp", None),
            P("fsdp", "sp"),
            P("fsdp"),
            P("fsdp"),
            P("fsdp", None),
            P("fsdp"),
            P("fsdp"),
            P("fsdp", None),
            P("fsdp"),
            P("fsdp"),
            P("fsdp"),
            P("fsdp", None),
            P("fsdp"),
            P("fsdp", None),
            P("fsdp"),
            P("fsdp", "sp", None),
        ),
        out_specs=(
            P("fsdp", "sp", None),
            P("fsdp", "sp", None),
            P("fsdp"),
            P("fsdp"),
            P("fsdp", None),
            P("fsdp"),
            P("fsdp"),
            P("fsdp", None),
            P("fsdp"),
            P("fsdp"),
            P("fsdp"),
            P("fsdp", None),
            P("fsdp"),
            P("fsdp", None),
            P("fsdp"),
        ),
        check_vma=False,
    )
```

profile of v0, /device:TPU:0, one launch (start us, length us, event | category | flops | bytes accessed | tf_op | source)
XLA Modules:
  0.0 666.2 jit_solution(9742364295532393877)
XLA Ops:
  18.1 26.8 %all-reduce.20 = (bf16[768]{0:T(1024)(128)(2,1)S(1)}, bf16[768]{0:T(1024)(128)(2,1)S(1)}, bf16[768]{0:T(1024)(128)(2,1)S(1)}, bf16[768]{0:T(1024)(128)(2,1)S(1)}...) all-reduce(bf16[768]{0:T(1024)(128)(2,1)S(1)} %dynamic-update-slice, ...), channel_id=1, replica_groups=mesh['fsdp'=8,'sp'=4] {'fsdp'}, use_global_device_ids=true, to_apply=%add.1 | all-reduce | flops 6144 | bytes 24576
  72.5 56.1 %all_gather.53 = s32[2,1024]{1,0:T(2,128)S(1)} all-gather(s32[2,256]{1,0:T(2,128)S(1)} %copy-done.41), channel_id=1, replica_groups=mesh['fsdp'=8,'sp'=4] {'sp'}, dimensions={1}, use_global_device_ids=true | all-gather | bytes 10240 | tf_op jit(solution)/shard_map/all_gather | solution.py:109
  138.1 47.1 %while.22 = (s32[]{:T(128)}, bf16[2,3,64,1024]{3,2,1,0:T(8,128)(2,1)}, f32[2,3,1024,1]{2,1,3,0:T(4,128)S(1)}, bf16[2,3,3,64,1024]{4,3,2,1,0:T(8,128)(2,1)}, s32[...) while((s32[]{:T(128)}, bf16[2,3,64,1024]{3,2,1,0:T(8,128)(2,1)}, ...), condition=%wide.region_5.6_spmd, body=%wide.region_2.5_spmd.sunk | while | flops 844297216 | bytes 93973664 | solution.py:129
  152.1 9.5 %fusion.111 = bf16[2,3,64,1024]{3,2,1,0:T(8,128)(2,1)} fusion(bf16[2,3,64,1024]{3,2,1,0:T(8,128)(2,1)} %get-tuple-element.279, s32[]{:T(128)S(6)} %copy.119, f32[3,1024,1024]{1,2,0:T(8,128)} %copy-done.4, f32[3,1024]{1,0:T(4,128)S(1)} %fusion.110, f32[3,1024]{1,0:T(4,128)S(1)} %get-tuple-element.260, pred[1024,1024]{0,1:T(8,128)(4,1)} %broadcast_compare_fusion.4, ...), kind=kOutput, calls=%fused_computation.9.clone.1 | convolution fusion | flops 418578432 | bytes 14444032 | tf_op jit(solution)/shard_map/while/body/eval_jaxpr/hqk,hdk->hdq/dot_general | solution.py:126
  175.7 9.4 %fusion.111 = bf16[2,3,64,1024]{3,2,1,0:T(8,128)(2,1)} fusion(bf16[2,3,64,1024]{3,2,1,0:T(8,128)(2,1)} %get-tuple-element.279, s32[]{:T(128)S(6)} %copy.119, f32[3,1024,1024]{1,2,0:T(8,128)} %copy-done.4, f32[3,1024]{1,0:T(4,128)S(1)} %fusion.110, f32[3,1024]{1,0:T(4,128)S(1)} %get-tuple-element.260, pred[1024,1024]{0,1:T(8,128)(4,1)} %broadcast_compare_fusion.4, ...), kind=kOutput, calls=%fused_computation.9.clone.1 | convolution fusion | flops 418578432 | bytes 14444032 | tf_op jit(solution)/shard_map/while/body/eval_jaxpr/hqk,hdk->hdq/dot_general | solution.py:126
  192.5 9.3 %all-gather = bf16[8,1,384]{2,1,0:T(2,128)(2,1)S(1)} all-gather(bf16[1,1,384]{2,1,0:T(2,128)(2,1)S(1)} %reshape.365), channel_id=1, replica_groups=mesh['fsdp'=8,'sp'=4] {'fsdp'}, dimensions={0}, use_global_device_ids=true | all-gather | bytes 6912 | tf_op jit(solution)/shard_map/all_gather | solution.py:105
  211.0 7.4 %fusion.72 = f32[512,3072]{1,0:T(8,128)} fusion(bf16[768,3072]{1,0:T(8,128)(2,1)} %all-gather.10.cloned.1.call-done, f32[512,768]{1,0:T(8,128)S(1)} %get-tuple-element.186, f32[768]{0:T(1024)S(1)} %convert_element_type.118, f32[768]{0:T(1024)S(1)} %convert_element_type.117, f32[512]{0:T(512)S(1)} %add_rsqrt_fusion, f32[512]{0:T(512)S(1)} %broadcast_multiply_fusion.4), kind=kOutput, calls=%fused_computation.120 | convolution fusion | flops 2417885184 | bytes 12593152 | tf_op jit(solution)/shard_map/dot_general | solution.py:137
  218.4 9.4 %convert_reduce_fusion = (f32[3072]{0:T(1024)}, bf16[512,3072]{1,0:T(8,128)(2,1)S(1)}) fusion(f32[512,3072]{1,0:T(8,128)} %fusion.72, f32[3072]{0:T(1024)S(1)} %bitcast.224, bf16[512,768]{1,0:T(8,128)(2,1)S(1)} %bitcast.210, bf16[3072,768]{1,0:T(8,128)(2,1)} %all-gather.12.cloned.1.call-done), kind=kOutput, calls=%fused_computation.64 | convolution fusion | flops 2450519040 | bytes 14966784 | tf_op jit(solution)/shard_map/dot_general | solution.py:42
  234.9 7.2 %fusion.71 = f32[768,3072]{1,0:T(8,128)} fusion(bf16[512,3072]{1,0:T(8,128)(2,1)} %copy-done.45, f32[512,768]{1,0:T(8,128)S(1)} %get-tuple-element.186, f32[768]{0:T(1024)S(1)} %convert_element_type.118, f32[768]{0:T(1024)S(1)} %convert_element_type.117, f32[512]{0:T(512)S(1)} %add_rsqrt_fusion, f32[512]{0:T(512)S(1)} %broadcast_multiply_fusion.4), kind=kOutput, calls=%fused_computation.119 | convolution fusion | flops 2417885184 | bytes 14166016 | tf_op jit(solution)/shard_map/dot_general | solution.py:42
  249.9 10.3 %fusion.73 = f32[3072,768]{1,0:T(8,128)} fusion(bf16[512,768]{1,0:T(8,128)(2,1)S(1)} %bitcast.211, f32[512,3072]{1,0:T(8,128)} %fusion.72, f32[3072]{0:T(1024)S(1)} %bitcast.225), kind=kOutput, calls=%fused_computation.121 | convolution fusion | flops 2431647744 | bytes 16527360 | tf_op jit(solution)/shard_map/dot_general | solution.py:42
  260.2 6.6 all-to-all-done.2
  268.1 75.5 %while.23 = (s32[]{:T(128)}, bf16[2,3,3,64,1024]{4,3,2,0,1:T(8,128)(2,1)}, bf16[2,3,3,64,1024]{4,3,2,1,0:T(8,128)(2,1)}, s32[2,1024]{1,0:T(2,128)S(1)}, f32[2,3,...) while((s32[]{:T(128)}, ...), condition=%wide.region_12.13_spmd, body=%wide.region_10.12_spmd.sunk | while | flops 2066019328 | bytes 260152704 | solution.py:190
  280.2 9.3 %multiply_reduce_fusion.7 = (f32[3,1024]{1,0:T(4,128)S(1)}, f32[3,1024,1024]{1,2,0:T(8,128)S(1)}) fusion(f32[3,1024,1024]{1,2,0:T(8,128)} %copy-done, f32[3,1024]{1,0:T(4,128)S(1)} %dynamic-slice_bitcast_fusion.26, pred[1024,1024]{0,1:T(8,128)(4,1)} %copy-done.3, bf16[2,3,3,64,1024]{4,3,2,1,0:T(8,128)(2,1)} %get-tuple-element.318, s32[]{:T(128)S(6)} %copy.127, ...), kind=kOutput, calls=%fused_computation.21.clone.1 | convolution fusion | flops 418378752 | bytes 27026944 | tf_op jit(solution)/shard_map/while/body/eval_jaxpr/hdq,hdk->hqk/dot_general | solution.py:179
  289.4 6.4 multiply_convert_fusion.5
  318.1 9.9 %multiply_reduce_fusion.7 = (f32[3,1024]{1,0:T(4,128)S(1)}, f32[3,1024,1024]{1,2,0:T(8,128)S(1)}) fusion(f32[3,1024,1024]{1,2,0:T(8,128)} %copy-done, f32[3,1024]{1,0:T(4,128)S(1)} %dynamic-slice_bitcast_fusion.26, pred[1024,1024]{0,1:T(8,128)(4,1)} %copy-done.3, bf16[2,3,3,64,1024]{4,3,2,1,0:T(8,128)(2,1)} %get-tuple-element.318, s32[]{:T(128)S(6)} %copy.127, ...), kind=kOutput, calls=%fused_computation.21.clone.1 | convolution fusion | flops 418378752 | bytes 27026944 | tf_op jit(solution)/shard_map/while/body/eval_jaxpr/hdq,hdk->hqk/dot_general | solution.py:179
  328.0 6.4 multiply_convert_fusion.5
  343.6 8.7 %copy.87 = bf16[3,1,192,2,1024]{2,3,0,1,4:T(2,128)(2,1)} copy(bf16[3,1,192,2,1024]{4,2,3,0,1:T(8,128)(2,1)} %bitcast.212) | data formatting | bytes 4718592 | tf_op jit(solution)/shard_map/reshape | solution.py:191
  358.5 68.2 %all-to-all-done.3 = bf16[3,1,192,2,1024]{2,3,0,1,4:T(2,128)(2,1)} async-done(((bf16[3,1,192,2,1024]{2,3,0,1,4:T(2,128)(2,1)}), bf16[3,1,192,2,1024]{2,3,0,1,4:T(2,128)(2,1)}, u32[]{:S(2)}, u32[]{:S(2)}) %all-to-all-start.3) | async-done | bytes 2359328 | tf_op jit(solution)/shard_map/all_to_all | solution.py:194
  426.6 8.5 %copy.98 = bf16[3,1,192,2,4,256]{5,4,2,3,0,1:T(4,128)(2,1)S(1)} copy(bf16[3,1,192,2,4,256]{2,3,0,5,4,1:T(2,128)(2,1)} %bitcast.34) | data formatting | bytes 4718592 | tf_op jit(solution)/shard_map/all_to_all | solution.py:194
  444.7 71.6 %reduce-scatter.5.cloned.1.call-done = f32[96,2304]{1,0:T(8,128)} async-done(((f32[768,2304]{1,0:T(8,128)}), f32[96,2304]{1,0:T(8,128)}) %reduce-scatter.5.cloned.1.call-update) | async-done | bytes 884752 | tf_op jit(solution)/shard_map/reduce_scatter | solution.py:208
  519.0 9.4 %add_convert_fusion = bf16[512,768]{1,0:T(8,128)(2,1)} fusion(f32[512,768]{1,0:T(8,128)} %copy-done.13, bf16[3072,768]{1,0:T(8,128)(2,1)} %all-gather.12.cloned.1.call-done, f32[768]{0:T(1024)S(1)} %convert_element_type.122, f32[512,3072]{1,0:T(8,128)} %fusion.72, f32[3072]{0:T(1024)S(1)} %bitcast.226), kind=kOutput, calls=%fused_computation.98 | convolution fusion | flops 2432827392 | bytes 13384704 | tf_op jit(solution)/shard_map/dot_general | solution.py:141
  535.9 25.0 %all-reduce.17 = (f32[768]{0:T(1024)S(1)}, f32[768]{0:T(1024)S(1)}, f32[768]{0:T(1024)S(1)}, f32[768]{0:T(1024)S(1)}, f32[768]{0:T(1024)S(1)}, /*index=5*/f32[76...) all-reduce(f32[768]{0:T(1024)S(1)} %get-tuple-element.113, ...), channel_id=2, replica_groups=mesh['fsdp'=8,'sp'=4] {'fsdp'}, use_global_device_ids=true, to_apply=%region_16.17.clone | all-reduce | flops 9216 | bytes 73728
  561.6 13.3 %all-reduce.18 = (f32[96]{0:T(128)}, f32[96]{0:T(128)}, f32[96]{0:T(128)}, f32[96]{0:T(128)}, f32[96]{0:T(128)}, /*index=5*/f32[96]{0:T(128)}, f32[96]{0:T(128)}, f32[384]{0:T(512)}, f32[96]{0:T(128)}) all-reduce(f32[96]{0:T(128)S(1)} %dynamic-slice.9, f32[96]{0:T(128)S(1)} %dynamic-slice.11, ...), channel_id=1, replica_groups=mesh['fsdp'=8,'sp'=4] {'sp'}, use_global_device_ids=true, to_apply=%region_17.18 | all-reduce | flops 1152 | bytes 9216 | tf_op jit(solution)/shard_map/psum | solution.py:234
  578.0 75.3 %all-reduce.23.cloned.1.call-done = (f32[96,2304]{1,0:T(8,128)}, f32[96,768]{1,0:T(8,128)}, f32[96,3072]{1,0:T(8,128)}, f32[384,768]{1,0:T(8,128)}) async-done(((f32[96,2304]{1,0:T(8,128)}, f32[96,768]{1,0:T(8,128)}, f32[96,3072]{1,0:T(8,128)}, f32[384,768]{1,0:T(8,128)}), (f32[96,2304]{1,0:T(8,128)}, f32[96,768]{1,0:T(8,128)}, f32[96,3072]{1,0:T(8,128)}, ...) | async-done | bytes 3538960 | tf_op jit(solution)/shard_map/psum | solution.py:234
  (253 shorter events, 185.0 us)
Async XLA Ops:
  7.2 41.8 %copy-start.5 = (bf16[2,256,768]{2,1,0:T(8,128)(2,1)S(1)}, bf16[2,256,768]{2,1,0:T(8,128)(2,1)}, u32[]{:S(2)}) copy-start(bf16[2,256,768]{2,1,0:T(8,128)(2,1)} %param.20) | copy-start | bytes 2359300
  7.2 42.1 %all-gather.6.cloned.1.call-start = ((), (), s32[]{:S(2)}) async-start(), calls=%async_computation.8 | async-start | bytes 3981312 | tf_op jit(solution)/shard_map/all_gather | solution.py:97
  7.9 200.3 %all-gather.8.cloned.1.call-start = ((), (), s32[]{:S(2)}) async-start(), calls=%async_computation.9 | async-start | bytes 1327104 | tf_op jit(solution)/shard_map/all_gather | solution.py:100
  8.7 202.4 %all-gather.10.cloned.1.call-start = ((), (), s32[]{:S(2)}) async-start(), calls=%async_computation.10 | async-start | bytes 5308416 | tf_op jit(solution)/shard_map/all_gather | solution.py:104
  66.9 61.7 %all-to-all-start = ((bf16[3,4,192,2,256]{4,3,2,0,1:T(2,128)(2,1)}), bf16[3,4,192,2,256]{4,3,2,0,1:T(2,128)(2,1)S(1)}, u32[]{:S(2)}, u32[]{:S(2)}) async-start(bf16[3,4,192,2,256]{4,3,2,0,1:T(2,128)(2,1)} %copy.78), calls=%async_computation | async-start | bytes 4718592 | tf_op jit(solution)/shard_map/all_to_all | solution.py:116
  71.9 146.6 %all-gather.12.cloned.1.call-start = ((), (), s32[]{:S(2)}) async-start(), calls=%async_computation.11 | async-start | bytes 5308416 | tf_op jit(solution)/shard_map/all_gather | solution.py:106
  185.2 23.0 %copy-start.6 = (bf16[2,256,768]{2,1,0:T(8,128)(2,1)S(1)}, bf16[2,256,768]{2,1,0:T(8,128)(2,1)}, u32[]{:S(2)}) copy-start(bf16[2,256,768]{2,1,0:T(8,128)(2,1)} %param.20) | copy-start | bytes 2359300
  188.9 19.1 %all-to-all-start.1 = ((bf16[192,2,4,256]{3,1,0,2:T(2,128)(2,1)}), bf16[192,2,4,256]{3,1,0,2:T(2,128)(2,1)S(1)}, u32[]{:S(2)}, u32[]{:S(2)}) async-start(bf16[192,2,4,256]{3,1,0,2:T(2,128)(2,1)} %copy.81), calls=%async_computation.1 | async-start | bytes 1572864 | tf_op jit(solution)/shard_map/all_to_all | solution.py:131
  192.4 252.2 %reduce-scatter.7.cloned.1.call-start = ((), (), s32[]{:S(2)}) async-start(), calls=%async_computation.13 | async-start | bytes 2654208 | tf_op jit(solution)/shard_map/reduce_scatter | solution.py:211
  201.8 48.0 %copy-start.35 = (f32[8,1,384]{2,1,0:T(1,128)}, f32[8,1,384]{2,1,0:T(1,128)S(1)}, u32[]{:S(2)}) copy-start(f32[8,1,384]{2,1,0:T(1,128)S(1)} %convert_element_type.136) | copy-start | bytes 36868
  210.7 24.2 %copy-start.13 = (f32[512,768]{1,0:T(8,128)}, f32[512,768]{1,0:T(8,128)S(1)}, u32[]{:S(2)}) copy-start(f32[512,768]{1,0:T(8,128)S(1)} %get-tuple-element.186) | copy-start | bytes 4718596
  232.6 9.5 %copy-start.8 = (f32[512,768]{1,0:T(8,128)}, f32[512,768]{1,0:T(8,128)S(1)}, u32[]{:S(2)}) copy-start(f32[512,768]{1,0:T(8,128)S(1)} %get-tuple-element.174) | copy-start | bytes 4718596
  234.8 209.8 %reduce-scatter.9.cloned.1.call-start = ((), (), s32[]{:S(2)}) async-start(), calls=%async_computation.14 | async-start | bytes 10616832 | tf_op jit(solution)/shard_map/reduce_scatter | solution.py:215
  246.1 20.6 %all-to-all-start.2 = ((bf16[768,2,1,256]{3,1,2,0:T(2,128)(2,1)}), bf16[768,2,1,256]{3,1,2,0:T(2,128)(2,1)S(1)}, u32[]{:S(2)}, u32[]{:S(2)}) async-start(bf16[768,2,1,256]{3,1,2,0:T(2,128)(2,1)} %copy.82), calls=%async_computation.2 | async-start | bytes 1572864 | tf_op jit(solution)/shard_map/all_to_all | solution.py:170
  249.6 195.1 %reduce-scatter.11.cloned.1.call-start = ((), (), s32[]{:S(2)}) async-start(), calls=%async_computation.15 | async-start | bytes 10616832 | tf_op jit(solution)/shard_map/reduce_scatter | solution.py:217
  318.1 9.9 %copy-start.1 = (f32[3,1024,1024]{1,2,0:T(8,128)S(1)}, f32[3,1024,1024]{1,2,0:T(8,128)}, u32[]{:S(2)}) copy-start(f32[3,1024,1024]{1,2,0:T(8,128)} %copy-done) | copy-start | bytes 37748740 | tf_op jit(solution)/shard_map/while
  352.3 74.3 %all-to-all-start.3 = ((bf16[3,1,192,2,1024]{2,3,0,1,4:T(2,128)(2,1)}), bf16[3,1,192,2,1024]{2,3,0,1,4:T(2,128)(2,1)}, u32[]{:S(2)}, u32[]{:S(2)}) async-start(bf16[3,1,192,2,1024]{2,3,0,1,4:T(2,128)(2,1)} %copy.87), calls=%async_computation.3 | async-start | bytes 6291456 | tf_op jit(solution)/shard_map/all_to_all | solution.py:194
  357.1 159.2 %reduce-scatter.5.cloned.1.call-start = ((), (), s32[]{:S(2)}) async-start(), calls=%async_computation.12 | async-start | bytes 7962624 | tf_op jit(solution)/shard_map/reduce_scatter | solution.py:208
  444.5 71.8 %copy-start.42 = (bf16[768]{0:T(1024)(128)(2,1)S(1)}, bf16[768]{0:T(1024)(128)(2,1)}, u32[]{:S(2)}) copy-start(bf16[768]{0:T(1024)(128)(2,1)} %get-tuple-element.170) | copy-start | bytes 4612
  444.5 74.4 %copy-start.36 = (f32[8,1,384]{2,1,0:T(1,128)S(1)}, f32[8,1,384]{2,1,0:T(1,128)}, u32[]{:S(2)}) copy-start(f32[8,1,384]{2,1,0:T(1,128)} %copy-done.35) | copy-start | bytes 36868
  444.6 208.7 %all-reduce.23.cloned.1.call-start = ((), (), s32[]{:S(2)}) async-start(), calls=%async_computation.16 | async-start | bytes 7077888 | tf_op jit(solution)/shard_map/psum | solution.py:234
  518.9 10.5 %copy-start.31 = (f32[1,2,2,128]{3,1,2,0:T(2,128)S(1)}, f32[1,2,2,128]{3,1,2,0:T(2,128)}, u32[]{:S(2)}) copy-start(f32[1,2,2,128]{3,1,2,0:T(2,128)} %copy-done.30) | copy-start | bytes 6148
  518.9 10.5 %copy-start.33 = (f32[1,2,2,128]{3,1,2,0:T(2,128)S(1)}, f32[1,2,2,128]{3,1,2,0:T(2,128)}, u32[]{:S(2)}) copy-start(f32[1,2,2,128]{3,1,2,0:T(2,128)} %copy-done.32) | copy-start | bytes 6148
  529.5 45.4 %copy-start.9 = (f32[512,768]{1,0:T(8,128)S(1)}, f32[512,768]{1,0:T(8,128)}, u32[]{:S(2)}) copy-start(f32[512,768]{1,0:T(8,128)} %copy-done.8) | copy-start | bytes 4718596
  (44 other events, 192.6 us)
Sparse Core Ops, SparseCore 0:
  9.9 36.7 all-gather.5
  48.5 23.9 all-gather.7
  74.4 38.7 all-gather.9
  114.9 38.7 all-gather.11
  235.0 44.5 reduce-scatter.6
  282.9 76.8 reduce-scatter.8
  363.2 76.8 reduce-scatter.10
  444.7 71.6 reduce-scatter.4
  518.9 134.2 all-reduce.22
where the time goes:
time: 673 us; the launch traced here: 666 us
  waiting for transfers between devices  231 us (34%)
  matrix products  147 us (22%)
  blocking collectives  130 us (19%)
  local copies, waits for them, and re-layouts  86.6 us (13%)
  other arithmetic  37.1 us (6%)
  starting transfers between devices  17.2 us (3%)
  between operations  16.8 us (2%)
    psum x1, waiting for transfers between devices, per_device(): lax.psum((owned[0], owned[1], owned[2], owned[3], owned[4], owned[5], own...  75.3 us
    reduce_scatter x1, waiting for transfers between devices, per_device(): lax.psum_scatter(grad_proj, 'fsdp', scatter_dimension=0, tiled=True)  71.6 us
    all_to_all x1, waiting for transfers between devices, per_device(): lax.all_to_all(grad_proj_heads, 'sp', split_axis=4, concat_axis=1, tiled=...  68.2 us
    all_gather x1, blocking collectives, per_device(): blocks = lax.all_gather(block_ids, 'sp', axis=1, tiled=True)  56.1 us
    dot_general x10, matrix products, contract(): lax.dot_general(left, right, (((left_dim,), (right_dim,)), ((), ())), pre...  54 us
    unnamed x2, blocking collectives  51.7 us
    while x36, local copies, waits for them, and re-layouts  20.6 us
    dot_general x2, matrix products, attend_back(): jnp.einsum('hdq,hdk->hqk', grad_mix, triple[2], preferred_element_type=f32)  19.1 us
  transfers between devices with their start and end apart: 13, of which 5 were waited for; matrix products, arithmetic and copies ran while one was open for 34% of the time, Pallas kernels for 0%

commit v1 on v0

--- a/solution.py
+++ b/solution.py
@@ -10,6 +10,23 @@
 GELU_C = 0.7978845608028654
 GELU_A = 0.044715
 MASKED = -1e30
+
+
+def laid_out(blocks, dim):
+    shape = list(blocks.shape[1:])
+    shape[dim] *= blocks.shape[0]
+    return jnp.moveaxis(blocks, 0, dim).reshape(shape)
+
+
+def collect(x, axis, dim):
+    size = lax.axis_size(axis)
+    right = [(i, (i + 1) % size) for i in range(size)]
+    blocks = [x]
+    while len(blocks) < size:
+        blocks.append(lax.ppermute(blocks[-1], axis, right))
+    position = lax.axis_index(axis)
+    blocks = jnp.stack(blocks)[(position - jnp.arange(size)) % size]
+    return laid_out(blocks, dim)
 
 
 def norm_forward(rows, gain, shift):
@@ -106,7 +123,7 @@
         lax.all_gather(w_reduce, "fsdp", axis=0, tiled=True),
         lax.all_gather(reduce_bias, "fsdp", axis=0, tiled=True),
     )
-    blocks = lax.all_gather(block_ids, "sp", axis=1, tiled=True)
+    blocks = collect(block_ids, "sp", 1)
     resid = inputs.astype(f32).reshape(rows, width)
     normed_one, inv_one, pre_one = norm_forward(resid, gain_one.astype(f32), shift_one.astype(f32))
     normed_in = pre_one.astype(bf16)

time: 673 us -> 674 us (level)
  blocking collectives: 130 us -> 74.5 us
  waiting for transfers between devices: 231 us -> 271 us
  starting transfers between devices: 17.2 us -> 32.2 us
    all_gather x1 -> x0, blocking collectives: 56.1 us -> none  [per_device(): blocks = lax.all_gather(block_ids, 'sp', axis=1, tiled=True)]
    ppermute x0 -> x3, waiting for transfers between devices: none -> 42 us  [collect(): blocks.append(lax.ppermute(blocks[-1], axis, right))]
    ppermute x0 -> x3, starting transfers between devices: none -> 15 us  [collect(): blocks.append(lax.ppermute(blocks[-1], axis, right))]
  transfers between devices with their start and end apart: 13 -> 16, of which waited for: 5 -> 8; matrix products, arithmetic and copies ran while one was open for 34% -> 34% of each run, Pallas kernels for 0% -> 0%
where the time goes in v1:
time: 674 us; the launch traced here: 666 us
  waiting for transfers between devices  271 us (40%)
  matrix products  147 us (22%)
  local copies, waits for them, and re-layouts  87.1 us (13%)
  blocking collectives  74.5 us (11%)
  other arithmetic  37 us (5%)
  starting transfers between devices  32.2 us (5%)
  between operations  16.8 us (2%)
    psum x1, waiting for transfers between devices, per_device(): lax.psum((owned[0], owned[1], owned[2], owned[3], owned[4], owned[5], own...  75.3 us
    reduce_scatter x1, waiting for transfers between devices, per_device(): lax.psum_scatter(grad_proj, 'fsdp', scatter_dimension=0, tiled=True)  71.8 us
    all_to_all x1, waiting for transfers between devices, per_device(): lax.all_to_all(grad_proj_heads, 'sp', split_axis=4, concat_axis=1, tiled=...  68.1 us
    dot_general x10, matrix products, contract(): lax.dot_general(left, right, (((left_dim,), (right_dim,)), ((), ())), pre...  54.1 us
    unnamed x2, blocking collectives  51.7 us
    ppermute x3, waiting for transfers between devices, collect(): blocks.append(lax.ppermute(blocks[-1], axis, right))  42 us
    while x36, local copies, waits for them, and re-layouts  20.7 us
    dot_general x2, matrix products, attend_back(): jnp.einsum('hdq,hdk->hqk', grad_mix, triple[2], preferred_element_type=f32)  19 us
  transfers between devices with their start and end apart: 16, of which 8 were waited for; matrix products, arithmetic and copies ran while one was open for 34% of the time, Pallas kernels for 0%

profile of v1, /device:TPU:0, one launch (start us, length us, event | category | flops | bytes accessed | tf_op | source)
XLA Modules:
  0.0 666.4 jit_solution(5059913481879034670)
XLA Ops:
  18.1 26.8 %all-reduce.20 = (bf16[768]{0:T(1024)(128)(2,1)S(1)}, bf16[768]{0:T(1024)(128)(2,1)S(1)}, bf16[768]{0:T(1024)(128)(2,1)S(1)}, bf16[768]{0:T(1024)(128)(2,1)S(1)}...) all-reduce(bf16[768]{0:T(1024)(128)(2,1)S(1)} %dynamic-update-slice, ...), channel_id=1, replica_groups=mesh['fsdp'=8,'sp'=4] {'fsdp'}, use_global_device_ids=true, to_apply=%add.1 | all-reduce | flops 6144 | bytes 24576
  73.9 37.8 %collective-permute-done = s32[2,256]{1,0:T(2,128)S(1)} collective-permute-done((s32[2,256]{1,0:T(2,128)S(1)}, s32[2,256]{1,0:T(2,128)S(1)}, u32[]{:S(2)}, u32[]{:S(2)}) %collective-permute-start) | collective-permute-done | bytes 2080 | tf_op jit(solution)/shard_map/ppermute | solution.py:26
  111.7 10.3 %collective-permute-start.1 = (s32[2,256]{1,0:T(2,128)S(1)}, s32[2,256]{1,0:T(2,128)S(1)}, u32[]{:S(2)}, u32[]{:S(2)}) collective-permute-start(s32[2,256]{1,0:T(2,128)S(1)} %collective-permute-done), channel_id=1, source_target_pairs={{0,1},{1,2},{2,3},{3,0},{4,5},{5,6},{6,7},{7,4},{8,9},{9,10},{10,1... | collective-permute-start | bytes 6152 | tf_op jit(solution)/shard_map/ppermute | solution.py:26
  138.8 47.1 %while.22 = (s32[]{:T(128)}, bf16[2,3,64,1024]{3,2,1,0:T(8,128)(2,1)}, f32[2,3,1024,1]{2,1,3,0:T(4,128)S(1)}, bf16[2,3,3,64,1024]{4,3,2,1,0:T(8,128)(2,1)}, s32[...) while((s32[]{:T(128)}, bf16[2,3,64,1024]{3,2,1,0:T(8,128)(2,1)}, ...), condition=%wide.region_5.6_spmd, body=%wide.region_2.5_spmd.sunk | while | flops 844297216 | bytes 93973664 | solution.py:146
  152.9 9.4 %fusion.113 = bf16[2,3,64,1024]{3,2,1,0:T(8,128)(2,1)} fusion(bf16[2,3,64,1024]{3,2,1,0:T(8,128)(2,1)} %get-tuple-element.279, s32[]{:T(128)S(6)} %copy.119, f32[3,1024,1024]{1,2,0:T(8,128)} %copy-done.4, f32[3,1024]{1,0:T(4,128)S(1)} %fusion.112, f32[3,1024]{1,0:T(4,128)S(1)} %get-tuple-element.260, ...), kind=kOutput, calls=%fused_computation.10.clone.1 | convolution fusion | flops 418578432 | bytes 14444032 | tf_op jit(solution)/shard_map/while/body/eval_jaxpr/hqk,hdk->hdq/dot_general | solution.py:143
  176.4 9.4 %fusion.113 = bf16[2,3,64,1024]{3,2,1,0:T(8,128)(2,1)} fusion(bf16[2,3,64,1024]{3,2,1,0:T(8,128)(2,1)} %get-tuple-element.279, s32[]{:T(128)S(6)} %copy.119, f32[3,1024,1024]{1,2,0:T(8,128)} %copy-done.4, f32[3,1024]{1,0:T(4,128)S(1)} %fusion.112, f32[3,1024]{1,0:T(4,128)S(1)} %get-tuple-element.260, ...), kind=kOutput, calls=%fused_computation.10.clone.1 | convolution fusion | flops 418578432 | bytes 14444032 | tf_op jit(solution)/shard_map/while/body/eval_jaxpr/hqk,hdk->hdq/dot_general | solution.py:143
  193.3 9.4 %all-gather = bf16[8,1,384]{2,1,0:T(2,128)(2,1)S(1)} all-gather(bf16[1,1,384]{2,1,0:T(2,128)(2,1)S(1)} %reshape.426), channel_id=1, replica_groups=mesh['fsdp'=8,'sp'=4] {'fsdp'}, dimensions={0}, use_global_device_ids=true | all-gather | bytes 6912 | tf_op jit(solution)/shard_map/all_gather | solution.py:122
  211.3 7.4 %fusion.74 = f32[512,3072]{1,0:T(8,128)} fusion(bf16[768,3072]{1,0:T(8,128)(2,1)} %all-gather.10.cloned.1.call-done, f32[512,768]{1,0:T(8,128)S(1)} %get-tuple-element.186, f32[768]{0:T(1024)S(1)} %convert_element_type.118, f32[768]{0:T(1024)S(1)} %convert_element_type.117, f32[512]{0:T(512)S(1)} %add_rsqrt_fusion, f32[512]{0:T(512)S(1)} %broadcast_multiply_fusion.4), kind=kOutput, calls=%fused_computation.129 | convolution fusion | flops 2417885184 | bytes 12593152 | tf_op jit(solution)/shard_map/dot_general | solution.py:154
  218.7 9.4 %convert_reduce_fusion = (f32[3072]{0:T(1024)}, bf16[512,3072]{1,0:T(8,128)(2,1)S(1)}) fusion(f32[512,3072]{1,0:T(8,128)} %fusion.74, f32[3072]{0:T(1024)S(1)} %bitcast.234, bf16[512,768]{1,0:T(8,128)(2,1)S(1)} %bitcast.219, bf16[3072,768]{1,0:T(8,128)(2,1)} %all-gather.12.cloned.1.call-done), kind=kOutput, calls=%fused_computation.65 | convolution fusion | flops 2450519040 | bytes 14966784 | tf_op jit(solution)/shard_map/dot_general | solution.py:59
  235.2 7.2 %fusion.73 = f32[768,3072]{1,0:T(8,128)} fusion(bf16[512,3072]{1,0:T(8,128)(2,1)} %copy-done.45, f32[512,768]{1,0:T(8,128)S(1)} %get-tuple-element.186, f32[768]{0:T(1024)S(1)} %convert_element_type.118, f32[768]{0:T(1024)S(1)} %convert_element_type.117, f32[512]{0:T(512)S(1)} %add_rsqrt_fusion, f32[512]{0:T(512)S(1)} %broadcast_multiply_fusion.4), kind=kOutput, calls=%fused_computation.128 | convolution fusion | flops 2417885184 | bytes 14166016 | tf_op jit(solution)/shard_map/dot_general | solution.py:59
  250.3 10.3 %fusion.75 = f32[3072,768]{1,0:T(8,128)} fusion(bf16[512,768]{1,0:T(8,128)(2,1)S(1)} %bitcast.220, f32[512,3072]{1,0:T(8,128)} %fusion.74, f32[3072]{0:T(1024)S(1)} %bitcast.235), kind=kOutput, calls=%fused_computation.130 | convolution fusion | flops 2431647744 | bytes 16527360 | tf_op jit(solution)/shard_map/dot_general | solution.py:59
  268.1 75.4 %while.23 = (s32[]{:T(128)}, bf16[2,3,3,64,1024]{4,3,2,0,1:T(8,128)(2,1)}, bf16[2,3,3,64,1024]{4,3,2,1,0:T(8,128)(2,1)}, s32[2,1024]{1,0:T(2,128)S(1)}, f32[2,3,...) while((s32[]{:T(128)}, ...), condition=%wide.region_12.13_spmd, body=%wide.region_10.12_spmd.sunk | while | flops 2066019328 | bytes 260152704 | solution.py:207
  280.2 9.3 %multiply_reduce_fusion.7 = (f32[3,1024]{1,0:T(4,128)S(1)}, f32[3,1024,1024]{1,2,0:T(8,128)S(1)}) fusion(f32[3,1024,1024]{1,2,0:T(8,128)} %copy-done, f32[3,1024]{1,0:T(4,128)S(1)} %dynamic-slice_bitcast_fusion.26, pred[1024,1024]{0,1:T(8,128)(4,1)} %copy-done.3, bf16[2,3,3,64,1024]{4,3,2,1,0:T(8,128)(2,1)} %get-tuple-element.318, s32[]{:T(128)S(6)} %copy.127, ...), kind=kOutput, calls=%fused_computation.22.clone.1 | convolution fusion | flops 418378752 | bytes 27026944 | tf_op jit(solution)/shard_map/while/body/eval_jaxpr/hdq,hdk->hqk/dot_general | solution.py:196
  318.3 9.7 %multiply_reduce_fusion.7 = (f32[3,1024]{1,0:T(4,128)S(1)}, f32[3,1024,1024]{1,2,0:T(8,128)S(1)}) fusion(f32[3,1024,1024]{1,2,0:T(8,128)} %copy-done, f32[3,1024]{1,0:T(4,128)S(1)} %dynamic-slice_bitcast_fusion.26, pred[1024,1024]{0,1:T(8,128)(4,1)} %copy-done.3, bf16[2,3,3,64,1024]{4,3,2,1,0:T(8,128)(2,1)} %get-tuple-element.318, s32[]{:T(128)S(6)} %copy.127, ...), kind=kOutput, calls=%fused_computation.22.clone.1 | convolution fusion | flops 418378752 | bytes 27026944 | tf_op jit(solution)/shard_map/while/body/eval_jaxpr/hdq,hdk->hqk/dot_general | solution.py:196
  328.0 6.4 multiply_convert_fusion.5
  343.6 8.7 %copy.87 = bf16[3,1,192,2,1024]{2,3,0,1,4:T(2,128)(2,1)} copy(bf16[3,1,192,2,1024]{4,2,3,0,1:T(8,128)(2,1)} %bitcast.221) | data formatting | bytes 4718592 | tf_op jit(solution)/shard_map/reshape | solution.py:208
  358.4 68.1 %all-to-all-done.3 = bf16[3,1,192,2,1024]{2,3,0,1,4:T(2,128)(2,1)} async-done(((bf16[3,1,192,2,1024]{2,3,0,1,4:T(2,128)(2,1)}), bf16[3,1,192,2,1024]{2,3,0,1,4:T(2,128)(2,1)}, u32[]{:S(2)}, u32[]{:S(2)}) %all-to-all-start.3) | async-done | bytes 2359328 | tf_op jit(solution)/shard_map/all_to_all | solution.py:211
  426.6 8.6 %copy.98 = bf16[3,1,192,2,4,256]{5,4,2,3,0,1:T(4,128)(2,1)S(1)} copy(bf16[3,1,192,2,4,256]{2,3,0,5,4,1:T(2,128)(2,1)} %bitcast.42) | data formatting | bytes 4718592 | tf_op jit(solution)/shard_map/all_to_all | solution.py:211
  444.6 71.8 %reduce-scatter.5.cloned.1.call-done = f32[96,2304]{1,0:T(8,128)} async-done(((f32[768,2304]{1,0:T(8,128)}), f32[96,2304]{1,0:T(8,128)}) %reduce-scatter.5.cloned.1.call-update) | async-done | bytes 884752 | tf_op jit(solution)/shard_map/reduce_scatter | solution.py:225
  519.1 9.4 %add_convert_fusion = bf16[512,768]{1,0:T(8,128)(2,1)} fusion(f32[512,768]{1,0:T(8,128)} %copy-done.13, bf16[3072,768]{1,0:T(8,128)(2,1)} %all-gather.12.cloned.1.call-done, f32[768]{0:T(1024)S(1)} %convert_element_type.122, f32[512,3072]{1,0:T(8,128)} %fusion.74, f32[3072]{0:T(1024)S(1)} %bitcast.236), kind=kOutput, calls=%fused_computation.99 | convolution fusion | flops 2432827392 | bytes 13384704 | tf_op jit(solution)/shard_map/dot_general | solution.py:158
  529.7 6.4 fusion.65
  536.1 25.0 %all-reduce.17 = (f32[768]{0:T(1024)S(1)}, f32[768]{0:T(1024)S(1)}, f32[768]{0:T(1024)S(1)}, f32[768]{0:T(1024)S(1)}, f32[768]{0:T(1024)S(1)}, /*index=5*/f32[76...) all-reduce(f32[768]{0:T(1024)S(1)} %get-tuple-element.113, ...), channel_id=2, replica_groups=mesh['fsdp'=8,'sp'=4] {'fsdp'}, use_global_device_ids=true, to_apply=%region_16.17.clone | all-reduce | flops 9216 | bytes 73728
  561.7 13.3 %all-reduce.18 = (f32[96]{0:T(128)}, f32[96]{0:T(128)}, f32[96]{0:T(128)}, f32[96]{0:T(128)}, f32[96]{0:T(128)}, /*index=5*/f32[96]{0:T(128)}, f32[96]{0:T(128)}, f32[384]{0:T(512)}, f32[96]{0:T(128)}) all-reduce(f32[96]{0:T(128)S(1)} %dynamic-slice.9, f32[96]{0:T(128)S(1)} %dynamic-slice.11, ...), channel_id=1, replica_groups=mesh['fsdp'=8,'sp'=4] {'sp'}, use_global_device_ids=true, to_apply=%region_17.18 | all-reduce | flops 1152 | bytes 9216 | tf_op jit(solution)/shard_map/psum | solution.py:251
  578.2 75.3 %all-reduce.23.cloned.1.call-done = (f32[96,2304]{1,0:T(8,128)}, f32[96,768]{1,0:T(8,128)}, f32[96,3072]{1,0:T(8,128)}, f32[384,768]{1,0:T(8,128)}) async-done(((f32[96,2304]{1,0:T(8,128)}, f32[96,768]{1,0:T(8,128)}, f32[96,3072]{1,0:T(8,128)}, f32[384,768]{1,0:T(8,128)}), (f32[96,2304]{1,0:T(8,128)}, f32[96,768]{1,0:T(8,128)}, f32[96,3072]{1,0:T(8,128)}, ...) | async-done | bytes 3538960 | tf_op jit(solution)/shard_map/psum | solution.py:251
  (262 shorter events, 199.8 us)
Async XLA Ops:
  7.2 41.7 %copy-start.5 = (bf16[2,256,768]{2,1,0:T(8,128)(2,1)S(1)}, bf16[2,256,768]{2,1,0:T(8,128)(2,1)}, u32[]{:S(2)}) copy-start(bf16[2,256,768]{2,1,0:T(8,128)(2,1)} %param.20) | copy-start | bytes 2359300
  7.2 42.1 %all-gather.6.cloned.1.call-start = ((), (), s32[]{:S(2)}) async-start(), calls=%async_computation.8 | async-start | bytes 3981312 | tf_op jit(solution)/shard_map/all_gather | solution.py:114
  7.9 200.5 %all-gather.8.cloned.1.call-start = ((), (), s32[]{:S(2)}) async-start(), calls=%async_computation.9 | async-start | bytes 1327104 | tf_op jit(solution)/shard_map/all_gather | solution.py:117
  8.7 202.6 %all-gather.10.cloned.1.call-start = ((), (), s32[]{:S(2)}) async-start(), calls=%async_computation.10 | async-start | bytes 5308416 | tf_op jit(solution)/shard_map/all_gather | solution.py:121
  66.9 62.6 %all-to-all-start = ((bf16[3,4,192,2,256]{4,3,2,0,1:T(2,128)(2,1)}), bf16[3,4,192,2,256]{4,3,2,0,1:T(2,128)(2,1)S(1)}, u32[]{:S(2)}, u32[]{:S(2)}) async-start(bf16[3,4,192,2,256]{4,3,2,0,1:T(2,128)(2,1)} %copy.78), calls=%async_computation | async-start | bytes 4718592 | tf_op jit(solution)/shard_map/all_to_all | solution.py:133
  71.8 146.9 %all-gather.12.cloned.1.call-start = ((), (), s32[]{:S(2)}) async-start(), calls=%async_computation.11 | async-start | bytes 5308416 | tf_op jit(solution)/shard_map/all_gather | solution.py:123
  71.8 39.8 %collective-permute-start = (s32[2,256]{1,0:T(2,128)S(1)}, s32[2,256]{1,0:T(2,128)S(1)}, u32[]{:S(2)}, u32[]{:S(2)}) collective-permute-start(s32[2,256]{1,0:T(2,128)S(1)} %copy-done.42), channel_id=1, source_target_pairs={{0,1},{1,2},{2,3},{3,0},{4,5},{5,6},{6,7},{7,4},{8,9},{9,10},{10,1... | collective-permute-start | bytes 6152 | tf_op jit(solution)/shard_map/ppermute | solution.py:26
  111.7 11.7 %collective-permute-start.1 = (s32[2,256]{1,0:T(2,128)S(1)}, s32[2,256]{1,0:T(2,128)S(1)}, u32[]{:S(2)}, u32[]{:S(2)}) collective-permute-start(s32[2,256]{1,0:T(2,128)S(1)} %collective-permute-done), channel_id=1, source_target_pairs={{0,1},{1,2},{2,3},{3,0},{4,5},{5,6},{6,7},{7,4},{8,9},{9,10},{10,1... | collective-permute-start | bytes 6152 | tf_op jit(solution)/shard_map/ppermute | solution.py:26
  123.3 5.6 collective-permute-start.2
  185.9 22.6 %copy-start.6 = (bf16[2,256,768]{2,1,0:T(8,128)(2,1)S(1)}, bf16[2,256,768]{2,1,0:T(8,128)(2,1)}, u32[]{:S(2)}) copy-start(bf16[2,256,768]{2,1,0:T(8,128)(2,1)} %param.20) | copy-start | bytes 2359300
  189.6 18.6 %all-to-all-start.1 = ((bf16[192,2,4,256]{3,1,0,2:T(2,128)(2,1)}), bf16[192,2,4,256]{3,1,0,2:T(2,128)(2,1)S(1)}, u32[]{:S(2)}, u32[]{:S(2)}) async-start(bf16[192,2,4,256]{3,1,0,2:T(2,128)(2,1)} %copy.81), calls=%async_computation.1 | async-start | bytes 1572864 | tf_op jit(solution)/shard_map/all_to_all | solution.py:148
  193.2 251.4 %reduce-scatter.7.cloned.1.call-start = ((), (), s32[]{:S(2)}) async-start(), calls=%async_computation.13 | async-start | bytes 2654208 | tf_op jit(solution)/shard_map/reduce_scatter | solution.py:228
  202.7 47.6 %copy-start.35 = (f32[8,1,384]{2,1,0:T(1,128)}, f32[8,1,384]{2,1,0:T(1,128)S(1)}, u32[]{:S(2)}) copy-start(f32[8,1,384]{2,1,0:T(1,128)S(1)} %convert_element_type.136) | copy-start | bytes 36868
  210.9 24.2 %copy-start.13 = (f32[512,768]{1,0:T(8,128)}, f32[512,768]{1,0:T(8,128)S(1)}, u32[]{:S(2)}) copy-start(f32[512,768]{1,0:T(8,128)S(1)} %get-tuple-element.186) | copy-start | bytes 4718596
  235.1 209.5 %reduce-scatter.9.cloned.1.call-start = ((), (), s32[]{:S(2)}) async-start(), calls=%async_computation.14 | async-start | bytes 10616832 | tf_op jit(solution)/shard_map/reduce_scatter | solution.py:232
  246.5 20.4 %all-to-all-start.2 = ((bf16[768,2,1,256]{3,1,2,0:T(2,128)(2,1)}), bf16[768,2,1,256]{3,1,2,0:T(2,128)(2,1)S(1)}, u32[]{:S(2)}, u32[]{:S(2)}) async-start(bf16[768,2,1,256]{3,1,2,0:T(2,128)(2,1)} %copy.82), calls=%async_computation.2 | async-start | bytes 1572864 | tf_op jit(solution)/shard_map/all_to_all | solution.py:187
  250.0 194.6 %reduce-scatter.11.cloned.1.call-start = ((), (), s32[]{:S(2)}) async-start(), calls=%async_computation.15 | async-start | bytes 10616832 | tf_op jit(solution)/shard_map/reduce_scatter | solution.py:234
  352.3 74.3 %all-to-all-start.3 = ((bf16[3,1,192,2,1024]{2,3,0,1,4:T(2,128)(2,1)}), bf16[3,1,192,2,1024]{2,3,0,1,4:T(2,128)(2,1)}, u32[]{:S(2)}, u32[]{:S(2)}) async-start(bf16[3,1,192,2,1024]{2,3,0,1,4:T(2,128)(2,1)} %copy.87), calls=%async_computation.3 | async-start | bytes 6291456 | tf_op jit(solution)/shard_map/all_to_all | solution.py:211
  357.1 159.4 %reduce-scatter.5.cloned.1.call-start = ((), (), s32[]{:S(2)}) async-start(), calls=%async_computation.12 | async-start | bytes 7962624 | tf_op jit(solution)/shard_map/reduce_scatter | solution.py:225
  444.5 72.0 %copy-start.41 = (bf16[768]{0:T(1024)(128)(2,1)S(1)}, bf16[768]{0:T(1024)(128)(2,1)}, u32[]{:S(2)}) copy-start(bf16[768]{0:T(1024)(128)(2,1)} %get-tuple-element.170) | copy-start | bytes 4612
  444.5 74.6 %copy-start.36 = (f32[8,1,384]{2,1,0:T(1,128)S(1)}, f32[8,1,384]{2,1,0:T(1,128)}, u32[]{:S(2)}) copy-start(f32[8,1,384]{2,1,0:T(1,128)} %copy-done.35) | copy-start | bytes 36868
  444.5 208.9 %all-reduce.23.cloned.1.call-start = ((), (), s32[]{:S(2)}) async-start(), calls=%async_computation.16 | async-start | bytes 7077888 | tf_op jit(solution)/shard_map/psum | solution.py:251
  519.1 10.5 %copy-start.31 = (f32[1,2,2,128]{3,1,2,0:T(2,128)S(1)}, f32[1,2,2,128]{3,1,2,0:T(2,128)}, u32[]{:S(2)}) copy-start(f32[1,2,2,128]{3,1,2,0:T(2,128)} %copy-done.30) | copy-start | bytes 6148
  529.7 45.4 %copy-start.9 = (f32[512,768]{1,0:T(8,128)S(1)}, f32[512,768]{1,0:T(8,128)}, u32[]{:S(2)}) copy-start(f32[512,768]{1,0:T(8,128)} %copy-done.8) | copy-start | bytes 4718596
  (47 other events, 221.9 us)
Sparse Core Ops, SparseCore 0:
  9.9 36.7 all-gather.5
  48.5 23.9 all-gather.7
  74.4 38.7 all-gather.9
  114.9 38.7 all-gather.11
  235.2 44.9 reduce-scatter.6
  283.6 76.8 reduce-scatter.8
  363.9 76.8 reduce-scatter.10
  444.6 71.8 reduce-scatter.4
  519.1 134.2 all-reduce.22
